TPU v7x, 256 devices: a whole 4x4x8 slice. The times are simulated.
256 devices in a mesh: section: 8 (over x, y_hi), shard: 32 (over z, y_lo, core).
Axes of the slice: x: 4, y: 4 (y_hi: 2, y_lo: 2; y = y_hi * 2 + y_lo), z: 8, core: 2. Of those that a mesh axis runs over, the one named last changes fastest.
Arguments:
- rows: bfloat16 [8, 2048, 6144], P('section', 'shard'), may hold values from -6 to 6
- expert_ids: int32 [8, 2048, 2], P('section', 'shard'), may hold values from 0 to 7, all different within a row; in each aligned block of 64 rows (0 to 63, 64 to 127, ..., all dimensions but the last counted through in order) at most 18 rows name the same one
- gate_probs: float32 [8, 2048, 2], P('section', 'shard'), may hold values from 0.1 to 1
- w_gate: bfloat16 [8, 6144, 8192], P('section', None, 'shard'), may hold values from -0.078125 to 0.078125
- w_up: bfloat16 [8, 6144, 8192], P('section', None, 'shard'), may hold values from -0.078125 to 0.078125
- w_down: bfloat16 [8, 8192, 6144], P('section', 'shard'), may hold values from -0.0625 to 0.0625
Outputs:
- handed: bfloat16 [8, 2048, 6144], P('section', 'shard')
Inputs may be any that keep to these rules, and one draw needn't show every extreme that they name: `expert_ids`: within each section's block of 64 tokens of one shard index, no expert is named by more than 18 tokens, and each token names 2 different experts.
All inputs are finite; a program needn't handle non-finite values.
Results may differ from a plain program's by a relative error of at most 0.011.
Values may be sent and summed in bfloat16 or wider, within the bound.
A program may use at most 128 MiB of HBM per device.

v0:
```python
import jax
import jax.numpy as jnp
from jax import lax
from jax.sharding import PartitionSpec as P

CAP = 18


def from_behind(value, axis, steps):
    count = lax.axis_size(axis)
    pairs = [(source, (source + steps) % count) for source in range(count)]
    return lax.ppermute(value, axis, pairs)


def unpack_rows(slot_values, expert_out, capacity):
    marks = jnp.arange(capacity, dtype=jnp.float32)[:, None]
    placed = (slot_values[None, :] == marks).astype(jnp.bfloat16)
    return lax.dot_general(
        placed, expert_out, (((0,), (0,)), ((), ())), preferred_element_type=jnp.float32
    )


def on_device(rows, expert_ids, gate_probs, w_gate, w_up, w_down):
    tokens = rows[0]
    chosen_ids = expert_ids[0]
    probs = gate_probs[0]
    gate_w = w_gate[0]
    up_w = w_up[0]
    down_w = w_down[0]
    section_num = lax.axis_index("section")
    hit = chosen_ids == section_num
    routed = jnp.any(hit, axis=-1)
    weight = jnp.sum(jnp.where(hit, probs, jnp.float32(0.0)), axis=-1)
    slot = jnp.cumsum(routed.astype(jnp.int32)) - 1
    slot_values = jnp.where(routed, slot, -1).astype(jnp.float32)
    marks = jnp.arange(CAP, dtype=jnp.float32)[:, None]
    placed = (slot_values[None, :] == marks).astype(jnp.bfloat16)
    packed = jnp.dot(placed, tokens, preferred_element_type=jnp.float32).astype(jnp.bfloat16)
    piece = lax.all_gather(packed, "shard", axis=0, tiled=True)
    gate = jnp.dot(piece, gate_w, preferred_element_type=jnp.float32)
    upper = jnp.dot(piece, up_w, preferred_element_type=jnp.float32)
    hidden_all = (jax.nn.silu(gate) * upper).astype(jnp.bfloat16)
    expert_out = lax.psum_scatter(
        jnp.dot(hidden_all, down_w, preferred_element_type=jnp.float32).astype(jnp.bfloat16),
        "shard",
        scatter_dimension=0,
        tiled=True,
    )
    per_token = unpack_rows(slot_values, expert_out, CAP)
    layer_out = (tokens.astype(jnp.float32) + weight[:, None] * per_token).astype(jnp.bfloat16)
    handed = from_behind(layer_out, "section", 1)
    return handed[None]


def solution(mesh):
    in_specs = (
        P("section", "shard", None),
        P("section", "shard", None),
        P("section", "shard", None),
        P("section", None, "shard"),
        P("section", None, "shard"),
        P("section", "shard", None),
    )
    out_specs = P("section", "shard", None)
    return jax.shard_map(
        on_device, mesh=mesh, in_specs=in_specs, out_specs=out_specs, check_vma=False
    )
```

profile of v0, /device:TPU:40, one launch (start us, length us, event | category | flops | bytes accessed | tf_op | source)
XLA Modules:
  0.0 356.0 jit_solution(13705711673027606384)
XLA Ops:
  7.7 2.1 fusion.3
  9.8 75.4 %all-gather.3.cloned.1.call-done = bf16[32,18,6144]{2,1,0:T(8,128)(2,1)} async-done(((bf16[1,18,6144]{2,1,0:T(8,128)(2,1)}), bf16[32,18,6144]{2,1,0:T(8,128)(2,1)}) %all-gather.3.cloned.1.call-update) | async-done | bytes 7077904 | tf_op jit(solution)/shard_map/all_gather | solution.py:39
  85.3 9.6 %reshape.43 = bf16[576,6144]{1,0:T(8,128)(2,1)} reshape(bf16[32,18,6144]{2,1,0:T(8,128)(2,1)} %all-gather.3.cloned.1.call-done) | data formatting | bytes 14155776
  94.9 6.0 %fusion.7 = f32[576,256]{1,0:T(8,128)S(1)} fusion(bf16[576,6144]{1,0:T(8,128)(2,1)} %reshape.43, bf16[1,6144,256]{2,1,0:T(8,128)(2,1)} %param.9), kind=kOutput, calls=%fused_computation.9 | convolution fusion | flops 1811939328 | bytes 10813440 | tf_op jit(solution)/shard_map/dot_general | solution.py:40
  101.7 2.0 fusion.12
  103.7 4.9 %convolution_convert_fusion = bf16[576,6144]{1,0:T(8,128)(2,1)} fusion(bf16[576,256]{1,0:T(8,128)(2,1)S(1)} %fusion.12, bf16[1,256,6144]{2,1,0:T(8,128)(2,1)S(1)} %copy-done), kind=kOutput, calls=%fused_computation | convolution fusion | flops 1815478272 | bytes 10518528 | tf_op jit(solution)/shard_map/dot_general | solution.py:44
  108.6 108.9 %fusion = bf16[24,6144]{1,0:T(8,128)(2,1)S(1)} fusion(bf16[576,6144]{1,0:T(8,128)(2,1)} %convolution_convert_fusion), kind=kCustom, calls=%all-reduce-scatter | all-reduce-scatter fusion | flops 4718593 | bytes 7373824
  217.5 1.9 collective-permute-start.1
  219.4 1.9 collective-permute-start.2
  221.4 3.0 collective-permute-start.8
  224.5 3.5 collective-permute-start.3
  228.0 3.1 collective-permute-start.4
  231.1 10.0 %collective-permute-done.8 = bf16[18,6144]{1,0:T(8,128)(2,1)S(1)} collective-permute-done((bf16[18,6144]{1,0:T(8,128)(2,1)S(1)}, bf16[18,6144]{1,0:T(8,128)(2,1)S(1)}, u32[]{:S(2)}, u32[]{:S(2)}) %collective-permute-start.8) | collective-permute-done | bytes 221216
  241.1 3.7 %collective-permute-start.5 = (bf16[24,6144]{1,0:T(8,128)(2,1)S(1)}, bf16[24,6144]{1,0:T(8,128)(2,1)}, u32[]{:S(2)}, u32[]{:S(2)}) collective-permute-start(bf16[24,6144]{1,0:T(8,128)(2,1)S(1)} %fusion), channel_id=1, source_target_pairs={{0,5},{1,6},{2,7},{3,8},{4,9},{5,10},{6,11},{7,12},{8,13},{9,14},{... | collective-permute-start | bytes 884744
  244.8 1.9 collective-permute-start.6
  246.8 7.8 %collective-permute-start.7 = (bf16[24,6144]{1,0:T(8,128)(2,1)S(1)}, bf16[24,6144]{1,0:T(8,128)(2,1)}, u32[]{:S(2)}, u32[]{:S(2)}) collective-permute-start(bf16[24,6144]{1,0:T(8,128)(2,1)S(1)} %fusion), channel_id=1, source_target_pairs={{0,7},{1,8},{2,9},{3,10},{4,11},{5,12},{6,13},{7,14},{8,15},{9,16}... | collective-permute-start | bytes 884744
  256.0 13.5 %collective-permute-done.4 = bf16[24,6144]{1,0:T(8,128)(2,1)} collective-permute-done((bf16[24,6144]{1,0:T(8,128)(2,1)S(1)}, bf16[24,6144]{1,0:T(8,128)(2,1)}, u32[]{:S(2)}, u32[]{:S(2)}) %collective-permute-start.4) | collective-permute-done | bytes 294944
  269.5 6.3 %collective-permute-done.5 = bf16[24,6144]{1,0:T(8,128)(2,1)} collective-permute-done((bf16[24,6144]{1,0:T(8,128)(2,1)S(1)}, bf16[24,6144]{1,0:T(8,128)(2,1)}, u32[]{:S(2)}, u32[]{:S(2)}) %collective-permute-start.5) | collective-permute-done | bytes 294944
  275.9 6.3 %collective-permute-done.6 = bf16[24,6144]{1,0:T(8,128)(2,1)} collective-permute-done((bf16[24,6144]{1,0:T(8,128)(2,1)S(1)}, bf16[24,6144]{1,0:T(8,128)(2,1)}, u32[]{:S(2)}, u32[]{:S(2)}) %collective-permute-start.6) | collective-permute-done | bytes 294944
  282.2 6.3 %collective-permute-done.7 = bf16[24,6144]{1,0:T(8,128)(2,1)} collective-permute-done((bf16[24,6144]{1,0:T(8,128)(2,1)S(1)}, bf16[24,6144]{1,0:T(8,128)(2,1)}, u32[]{:S(2)}, u32[]{:S(2)}) %collective-permute-start.7) | collective-permute-done | bytes 294944
  288.5 34.5 %concatenate = bf16[210,6144]{1,0:T(8,128)(2,1)} concatenate(bf16[18,6144]{1,0:T(8,128)(2,1)} %copy-done.4, bf16[24,6144]{1,0:T(8,128)(2,1)} %collective-permute-done.7, bf16[24,6144]{1,0:T(8,128)(2,1)} %collective-permute-done.6, bf16[24,6144]{1,0:T(8,128)(2,1)} %collective-permute-done.5, bf16[24,6144]{1,0:T(8,128)(2,1)} %collective-permute-done.4, ...), dimensions={0} | concatenate | bytes 5160960
  323.0 1.7 fusion.2
  324.7 2.2 collective-permute-start
  326.9 21.4 %collective-permute-done = bf16[64,6144]{1,0:T(8,128)(2,1)S(1)} collective-permute-done((bf16[64,6144]{1,0:T(8,128)(2,1)S(1)}, bf16[64,6144]{1,0:T(8,128)(2,1)S(1)}, u32[]{:S(2)}, u32[]{:S(2)}) %collective-permute-start) | collective-permute-done | bytes 786464 | tf_op jit(solution)/shard_map/ppermute | solution.py:12
  (33 shorter events, 3.6 us)
Async XLA Ops:
  6.5 97.1 %copy-start = (bf16[1,256,6144]{2,1,0:T(8,128)(2,1)S(1)}, bf16[1,256,6144]{2,1,0:T(8,128)(2,1)}, u32[]{:S(2)}) copy-start(bf16[1,256,6144]{2,1,0:T(8,128)(2,1)} %param.11) | copy-start | bytes 9437188
  6.5 78.7 %all-gather.3.cloned.1.call-start = ((), (), s32[]{:S(2)}) async-start(), calls=%async_computation | async-start | bytes 9732096 | tf_op jit(solution)/shard_map/all_gather | solution.py:39
  94.8 6.1 %copy-start.1 = (bf16[576,6144]{1,0:T(8,128)(2,1)S(1)}, bf16[576,6144]{1,0:T(8,128)(2,1)}, u32[]{:S(2)}) copy-start(bf16[576,6144]{1,0:T(8,128)(2,1)} %reshape.43) | copy-start | bytes 21233668
  94.8 6.8 %copy-start.8 = (bf16[1,6144,256]{2,1,0:T(8,128)(2,1)S(1)}, bf16[1,6144,256]{2,1,0:T(8,128)(2,1)}, u32[]{:S(2)}) copy-start(bf16[1,6144,256]{2,1,0:T(8,128)(2,1)} %param.10) | copy-start | bytes 9437188
  108.6 146.0 %copy-start.7 = (u32[256]{0:T(256)S(1)}, u32[256]{0:T(256)}, u32[]{:S(2)}) copy-start(u32[256]{0:T(256)} %constant.29) | copy-start | bytes 3076
  108.6 147.4 %copy-start.5 = (s32[1,64,2]{1,2,0:T(2,128)S(1)}, s32[1,64,2]{1,2,0:T(2,128)}, u32[]{:S(2)}) copy-start(s32[1,64,2]{1,2,0:T(2,128)} %param.7) | copy-start | bytes 1540
  108.6 147.4 %copy-start.6 = (f32[1,64,2]{1,2,0:T(2,128)S(1)}, f32[1,64,2]{1,2,0:T(2,128)}, u32[]{:S(2)}) copy-start(f32[1,64,2]{1,2,0:T(2,128)} %param.8) | copy-start | bytes 1540
  217.5 27.3 %collective-permute-start.1 = (bf16[24,6144]{1,0:T(8,128)(2,1)S(1)}, bf16[24,6144]{1,0:T(8,128)(2,1)S(1)}, u32[]{:S(2)}, u32[]{:S(2)}) collective-permute-start(bf16[24,6144]{1,0:T(8,128)(2,1)S(1)} %fusion), channel_id=1, source_target_pairs={{0,1},{1,2},{2,3},{3,4},{4,5},{5,6},{6,7},{7,8},{8,9},{9,10},{10,1... | collective-permute-start | bytes 884744
  219.4 27.3 %collective-permute-start.2 = (bf16[24,6144]{1,0:T(8,128)(2,1)S(1)}, bf16[24,6144]{1,0:T(8,128)(2,1)S(1)}, u32[]{:S(2)}, u32[]{:S(2)}) collective-permute-start(bf16[24,6144]{1,0:T(8,128)(2,1)S(1)} %fusion), channel_id=1, source_target_pairs={{0,2},{1,3},{2,4},{3,5},{4,6},{5,7},{6,8},{7,9},{8,10},{9,11},{10,... | collective-permute-start | bytes 884744
  221.4 19.7 %collective-permute-start.8 = (bf16[18,6144]{1,0:T(8,128)(2,1)S(1)}, bf16[18,6144]{1,0:T(8,128)(2,1)S(1)}, u32[]{:S(2)}, u32[]{:S(2)}) collective-permute-start(bf16[18,6144]{1,0:T(8,128)(2,1)S(1)} %slice), channel_id=1, source_target_pairs={{0,8},{1,9},{2,10},{3,11},{4,12},{5,13},{6,14},{7,15},{8,16},{9,17... | collective-permute-start | bytes 663560
  224.5 31.5 %collective-permute-start.3 = (bf16[24,6144]{1,0:T(8,128)(2,1)S(1)}, bf16[24,6144]{1,0:T(8,128)(2,1)}, u32[]{:S(2)}, u32[]{:S(2)}) collective-permute-start(bf16[24,6144]{1,0:T(8,128)(2,1)S(1)} %fusion), channel_id=1, source_target_pairs={{0,3},{1,4},{2,5},{3,6},{4,7},{5,8},{6,9},{7,10},{8,11},{9,12},{10... | collective-permute-start | bytes 884744
  228.0 41.5 %collective-permute-start.4 = (bf16[24,6144]{1,0:T(8,128)(2,1)S(1)}, bf16[24,6144]{1,0:T(8,128)(2,1)}, u32[]{:S(2)}, u32[]{:S(2)}) collective-permute-start(bf16[24,6144]{1,0:T(8,128)(2,1)S(1)} %fusion), channel_id=1, source_target_pairs={{0,4},{1,5},{2,6},{3,7},{4,8},{5,9},{6,10},{7,11},{8,12},{9,13},{1... | collective-permute-start | bytes 884744
  241.1 13.5 %copy-start.4 = (bf16[18,6144]{1,0:T(8,128)(2,1)}, bf16[18,6144]{1,0:T(8,128)(2,1)S(1)}, u32[]{:S(2)}) copy-start(bf16[18,6144]{1,0:T(8,128)(2,1)S(1)} %collective-permute-done.8) | copy-start | bytes 663556
  241.1 34.8 %collective-permute-start.5 = (bf16[24,6144]{1,0:T(8,128)(2,1)S(1)}, bf16[24,6144]{1,0:T(8,128)(2,1)}, u32[]{:S(2)}, u32[]{:S(2)}) collective-permute-start(bf16[24,6144]{1,0:T(8,128)(2,1)S(1)} %fusion), channel_id=1, source_target_pairs={{0,5},{1,6},{2,7},{3,8},{4,9},{5,10},{6,11},{7,12},{8,13},{9,14},{... | collective-permute-start | bytes 884744
  244.8 2.0 copy-start.2
  244.8 37.4 %collective-permute-start.6 = (bf16[24,6144]{1,0:T(8,128)(2,1)S(1)}, bf16[24,6144]{1,0:T(8,128)(2,1)}, u32[]{:S(2)}, u32[]{:S(2)}) collective-permute-start(bf16[24,6144]{1,0:T(8,128)(2,1)S(1)} %fusion), channel_id=1, source_target_pairs={{0,6},{1,7},{2,8},{3,9},{4,10},{5,11},{6,12},{7,13},{8,14},{9,15},... | collective-permute-start | bytes 884744
  246.7 7.8 %copy-start.3 = (bf16[24,6144]{1,0:T(8,128)(2,1)}, bf16[24,6144]{1,0:T(8,128)(2,1)S(1)}, u32[]{:S(2)}) copy-start(bf16[24,6144]{1,0:T(8,128)(2,1)S(1)} %collective-permute-done.2) | copy-start | bytes 884740
  246.8 41.7 %collective-permute-start.7 = (bf16[24,6144]{1,0:T(8,128)(2,1)S(1)}, bf16[24,6144]{1,0:T(8,128)(2,1)}, u32[]{:S(2)}, u32[]{:S(2)}) collective-permute-start(bf16[24,6144]{1,0:T(8,128)(2,1)S(1)} %fusion), channel_id=1, source_target_pairs={{0,7},{1,8},{2,9},{3,10},{4,11},{5,12},{6,13},{7,14},{8,15},{9,16}... | collective-permute-start | bytes 884744
  324.7 23.6 %collective-permute-start = (bf16[64,6144]{1,0:T(8,128)(2,1)S(1)}, bf16[64,6144]{1,0:T(8,128)(2,1)S(1)}, u32[]{:S(2)}, u32[]{:S(2)}) collective-permute-start(bf16[64,6144]{1,0:T(8,128)(2,1)S(1)} %fusion.2), channel_id=1, source_target_pairs={{0,32},{32,64},{64,96},{96,128},{128,160},{160,192},{192,224},{224... | collective-permute-start | bytes 2359304 | tf_op jit(solution)/shard_map/ppermute | solution.py:12
Sparse Core Ops, SparseCore 0:
  9.9 75.2 all-gather.2
where the time goes:
time: 359 us; the launch traced here: 356 us
  waiting for transfers between devices  139 us (39%)
  blocking collectives  109 us (30%)
  local copies, waits for them, and re-layouts  46.6 us (13%)
  starting transfers between devices  29.1 us (8%)
  matrix products  16.7 us (5%)
  between operations  14.3 us (4%)
    unnamed x1, blocking collectives  109 us
    all_gather x1, waiting for transfers between devices, on_device(): piece = lax.all_gather(packed, 'shard', axis=0, tiled=True)  75.4 us
    unnamed x23, local copies, waits for them, and re-layouts  46.5 us
    unnamed x9, waiting for transfers between devices  42.5 us
    unnamed x8, starting transfers between devices  26.9 us
    ppermute x1, waiting for transfers between devices, from_behind(): return lax.ppermute(value, axis, pairs)  21.4 us
  transfers between devices with their start and end apart: 10, of which 7 were waited for; matrix products, arithmetic and copies ran while one was open for 0% of the time, Pallas kernels for 0%

commit v1 on v0

--- a/solution.py
+++ b/solution.py
@@ -4,6 +4,13 @@
 from jax.sharding import PartitionSpec as P
 
 CAP = 18
+
+
+def all_by_exchange(value, name, dim):
+    n_dev = lax.axis_size(name)
+    tiles = jnp.stack([value for _ in range(n_dev)])
+    tiles = lax.all_to_all(tiles, name, split_axis=0, concat_axis=0)
+    return jnp.concatenate(tiles, axis=dim)
 
 
 def from_behind(value, axis, steps):
@@ -36,7 +43,7 @@
     marks = jnp.arange(CAP, dtype=jnp.float32)[:, None]
     placed = (slot_values[None, :] == marks).astype(jnp.bfloat16)
     packed = jnp.dot(placed, tokens, preferred_element_type=jnp.float32).astype(jnp.bfloat16)
-    piece = lax.all_gather(packed, "shard", axis=0, tiled=True)
+    piece = all_by_exchange(packed, "shard", 0)
     gate = jnp.dot(piece, gate_w, preferred_element_type=jnp.float32)
     upper = jnp.dot(piece, up_w, preferred_element_type=jnp.float32)
     hidden_all = (jax.nn.silu(gate) * upper).astype(jnp.bfloat16)

time: 359 us -> 487 us (1.36)
  blocking collectives: 109 us -> 326 us
  waiting for transfers between devices: 139 us -> 64 us
  between operations: 14.3 us -> 0.83 us
    all_to_all x0 -> x1, blocking collectives: none -> 217 us  [all_by_exchange(): tiles = lax.all_to_all(tiles, name, split_axis=0, concat_axis=0)]
    all_gather x1 -> x0, waiting for transfers between devices: 75.4 us -> none  [on_device(): piece = lax.all_gather(packed, 'shard', axis=0, tiled=True)]
    unnamed x23 -> x22, local copies, waits for them, and re-layouts: 46.5 us -> 36.7 us
    reshape x0 -> x1, local copies, waits for them, and re-layouts: none -> 9.61 us  [all_by_exchange(): return jnp.concatenate(tiles, axis=dim)]
    unnamed x9 -> x8, waiting for transfers between devices: 42.5 us -> 42.4 us
  transfers between devices with their start and end apart: 10 -> 9, of which waited for: 7 -> 6; matrix products, arithmetic and copies ran while one was open for 0% -> 0% of each run, Pallas kernels for 0% -> 0%
where the time goes in v1:
time: 487 us; the launch traced here: 484 us
  blocking collectives  326 us (67%)
  waiting for transfers between devices  64 us (13%)
  local copies, waits for them, and re-layouts  47.5 us (10%)
  starting transfers between devices  28.9 us (6%)
  matrix products  16 us (3%)
    all_to_all x1, blocking collectives, all_by_exchange(): tiles = lax.all_to_all(tiles, name, split_axis=0, concat_axis=0)  217 us
    unnamed x1, blocking collectives  108 us
    unnamed x8, waiting for transfers between devices  42.4 us
    unnamed x22, local copies, waits for them, and re-layouts  36.7 us
    unnamed x8, starting transfers between devices  26.5 us
    ppermute x1, waiting for transfers between devices, from_behind(): return lax.ppermute(value, axis, pairs)  21.7 us
  transfers between devices with their start and end apart: 9, of which 6 were waited for; matrix products, arithmetic and copies ran while one was open for 0% of the time, Pallas kernels for 0%

profile of v1, /device:TPU:40, one launch (start us, length us, event | category | flops | bytes accessed | tf_op | source)
XLA Modules:
  0.0 484.0 jit_solution(10935402019314050768)
XLA Ops:
  1.2 1.4 convolution_convert_fusion.1
  3.7 217.4 %all_to_all.5 = bf16[32,18,6144]{2,1,0:T(8,128)(2,1)} all-to-all(bf16[32,18,6144]{2,1,0:T(8,128)(2,1)S(1)} %stack.2), channel_id=1, replica_groups=mesh['section'=8,'shard'=32] {'shard'}, dimensions={0} | all-to-all | bytes 14155776 | tf_op jit(solution)/shard_map/all_to_all | solution.py:12
  221.1 9.6 %reshape.46 = bf16[576,6144]{1,0:T(8,128)(2,1)} reshape(bf16[32,18,6144]{2,1,0:T(8,128)(2,1)} %all_to_all.5) | data formatting | bytes 14155776 | tf_op jit(solution)/shard_map/reshape | solution.py:13
  230.7 6.0 %fusion.6 = f32[576,256]{1,0:T(8,128)S(1)} fusion(bf16[576,6144]{1,0:T(8,128)(2,1)} %reshape.46, bf16[1,6144,256]{2,1,0:T(8,128)(2,1)} %param.9), kind=kOutput, calls=%fused_computation.8 | convolution fusion | flops 1811939328 | bytes 10813440 | tf_op jit(solution)/shard_map/dot_general | solution.py:47
  237.5 2.0 fusion.11
  239.5 4.9 %convolution_convert_fusion = bf16[576,6144]{1,0:T(8,128)(2,1)} fusion(bf16[576,256]{1,0:T(8,128)(2,1)S(1)} %fusion.11, bf16[1,256,6144]{2,1,0:T(8,128)(2,1)S(1)} %copy-done), kind=kOutput, calls=%fused_computation | convolution fusion | flops 1815478272 | bytes 10518528 | tf_op jit(solution)/shard_map/dot_general | solution.py:51
  244.4 108.2 %fusion = bf16[24,6144]{1,0:T(8,128)(2,1)S(1)} fusion(bf16[576,6144]{1,0:T(8,128)(2,1)} %convolution_convert_fusion), kind=kCustom, calls=%all-reduce-scatter | all-reduce-scatter fusion | flops 4718593 | bytes 7373824
  352.7 1.9 collective-permute-start.1
  354.6 1.9 collective-permute-start.2
  356.6 3.0 collective-permute-start.8
  359.6 2.3 collective-permute-start.3
  362.0 3.2 collective-permute-start.4
  365.2 10.5 %collective-permute-done.8 = bf16[18,6144]{1,0:T(8,128)(2,1)S(1)} collective-permute-done((bf16[18,6144]{1,0:T(8,128)(2,1)S(1)}, bf16[18,6144]{1,0:T(8,128)(2,1)S(1)}, u32[]{:S(2)}, u32[]{:S(2)}) %collective-permute-start.8) | collective-permute-done | bytes 221216
  375.7 4.2 collective-permute-start.5
  379.9 1.9 collective-permute-start.6
  381.8 8.0 %collective-permute-start.7 = (bf16[24,6144]{1,0:T(8,128)(2,1)S(1)}, bf16[24,6144]{1,0:T(8,128)(2,1)}, u32[]{:S(2)}, u32[]{:S(2)}) collective-permute-start(bf16[24,6144]{1,0:T(8,128)(2,1)S(1)} %fusion), channel_id=1, source_target_pairs={{0,7},{1,8},{2,9},{3,10},{4,11},{5,12},{6,13},{7,14},{8,15},{9,16}... | collective-permute-start | bytes 884744
  391.2 12.9 %collective-permute-done.4 = bf16[24,6144]{1,0:T(8,128)(2,1)} collective-permute-done((bf16[24,6144]{1,0:T(8,128)(2,1)S(1)}, bf16[24,6144]{1,0:T(8,128)(2,1)}, u32[]{:S(2)}, u32[]{:S(2)}) %collective-permute-start.4) | collective-permute-done | bytes 294944
  404.1 6.3 %collective-permute-done.5 = bf16[24,6144]{1,0:T(8,128)(2,1)} collective-permute-done((bf16[24,6144]{1,0:T(8,128)(2,1)S(1)}, bf16[24,6144]{1,0:T(8,128)(2,1)}, u32[]{:S(2)}, u32[]{:S(2)}) %collective-permute-start.5) | collective-permute-done | bytes 294944
  410.4 6.3 %collective-permute-done.6 = bf16[24,6144]{1,0:T(8,128)(2,1)} collective-permute-done((bf16[24,6144]{1,0:T(8,128)(2,1)S(1)}, bf16[24,6144]{1,0:T(8,128)(2,1)}, u32[]{:S(2)}, u32[]{:S(2)}) %collective-permute-start.6) | collective-permute-done | bytes 294944
  416.7 6.3 %collective-permute-done.7 = bf16[24,6144]{1,0:T(8,128)(2,1)} collective-permute-done((bf16[24,6144]{1,0:T(8,128)(2,1)S(1)}, bf16[24,6144]{1,0:T(8,128)(2,1)}, u32[]{:S(2)}, u32[]{:S(2)}) %collective-permute-start.7) | collective-permute-done | bytes 294944
  423.1 34.3 %concatenate = bf16[210,6144]{1,0:T(8,128)(2,1)} concatenate(bf16[18,6144]{1,0:T(8,128)(2,1)} %copy-done.4, bf16[24,6144]{1,0:T(8,128)(2,1)} %collective-permute-done.7, bf16[24,6144]{1,0:T(8,128)(2,1)} %collective-permute-done.6, bf16[24,6144]{1,0:T(8,128)(2,1)} %collective-permute-done.5, bf16[24,6144]{1,0:T(8,128)(2,1)} %collective-permute-done.4, ...), dimensions={0} | concatenate | bytes 5160960
  457.4 1.7 fusion.2
  459.1 2.4 collective-permute-start
  461.4 21.7 %collective-permute-done = bf16[64,6144]{1,0:T(8,128)(2,1)S(1)} collective-permute-done((bf16[64,6144]{1,0:T(8,128)(2,1)S(1)}, bf16[64,6144]{1,0:T(8,128)(2,1)S(1)}, u32[]{:S(2)}, u32[]{:S(2)}) %collective-permute-start) | collective-permute-done | bytes 786464 | tf_op jit(solution)/shard_map/ppermute | solution.py:19
  (32 shorter events, 4.7 us)
Async XLA Ops:
  0.0 239.5 %copy-start = (bf16[1,256,6144]{2,1,0:T(8,128)(2,1)S(1)}, bf16[1,256,6144]{2,1,0:T(8,128)(2,1)}, u32[]{:S(2)}) copy-start(bf16[1,256,6144]{2,1,0:T(8,128)(2,1)} %param.11) | copy-start | bytes 9437188
  230.7 6.1 %copy-start.1 = (bf16[576,6144]{1,0:T(8,128)(2,1)S(1)}, bf16[576,6144]{1,0:T(8,128)(2,1)}, u32[]{:S(2)}) copy-start(bf16[576,6144]{1,0:T(8,128)(2,1)} %reshape.46) | copy-start | bytes 21233668
  230.7 6.8 %copy-start.8 = (bf16[1,6144,256]{2,1,0:T(8,128)(2,1)S(1)}, bf16[1,6144,256]{2,1,0:T(8,128)(2,1)}, u32[]{:S(2)}) copy-start(bf16[1,6144,256]{2,1,0:T(8,128)(2,1)} %param.10) | copy-start | bytes 9437188
  244.4 145.4 %copy-start.7 = (u32[256]{0:T(256)S(1)}, u32[256]{0:T(256)}, u32[]{:S(2)}) copy-start(u32[256]{0:T(256)} %constant.29) | copy-start | bytes 3076
  244.4 146.7 %copy-start.5 = (s32[1,64,2]{1,2,0:T(2,128)S(1)}, s32[1,64,2]{1,2,0:T(2,128)}, u32[]{:S(2)}) copy-start(s32[1,64,2]{1,2,0:T(2,128)} %param.7) | copy-start | bytes 1540
  244.4 146.7 %copy-start.6 = (f32[1,64,2]{1,2,0:T(2,128)S(1)}, f32[1,64,2]{1,2,0:T(2,128)}, u32[]{:S(2)}) copy-start(f32[1,64,2]{1,2,0:T(2,128)} %param.8) | copy-start | bytes 1540
  352.7 27.2 %collective-permute-start.1 = (bf16[24,6144]{1,0:T(8,128)(2,1)S(1)}, bf16[24,6144]{1,0:T(8,128)(2,1)S(1)}, u32[]{:S(2)}, u32[]{:S(2)}) collective-permute-start(bf16[24,6144]{1,0:T(8,128)(2,1)S(1)} %fusion), channel_id=1, source_target_pairs={{0,1},{1,2},{2,3},{3,4},{4,5},{5,6},{6,7},{7,8},{8,9},{9,10},{10,1... | collective-permute-start | bytes 884744
  354.6 27.2 %collective-permute-start.2 = (bf16[24,6144]{1,0:T(8,128)(2,1)S(1)}, bf16[24,6144]{1,0:T(8,128)(2,1)S(1)}, u32[]{:S(2)}, u32[]{:S(2)}) collective-permute-start(bf16[24,6144]{1,0:T(8,128)(2,1)S(1)} %fusion), channel_id=1, source_target_pairs={{0,2},{1,3},{2,4},{3,5},{4,6},{5,7},{6,8},{7,9},{8,10},{9,11},{10,... | collective-permute-start | bytes 884744
  356.6 19.1 %collective-permute-start.8 = (bf16[18,6144]{1,0:T(8,128)(2,1)S(1)}, bf16[18,6144]{1,0:T(8,128)(2,1)S(1)}, u32[]{:S(2)}, u32[]{:S(2)}) collective-permute-start(bf16[18,6144]{1,0:T(8,128)(2,1)S(1)} %slice), channel_id=1, source_target_pairs={{0,8},{1,9},{2,10},{3,11},{4,12},{5,13},{6,14},{7,15},{8,16},{9,17... | collective-permute-start | bytes 663560
  359.6 31.5 %collective-permute-start.3 = (bf16[24,6144]{1,0:T(8,128)(2,1)S(1)}, bf16[24,6144]{1,0:T(8,128)(2,1)}, u32[]{:S(2)}, u32[]{:S(2)}) collective-permute-start(bf16[24,6144]{1,0:T(8,128)(2,1)S(1)} %fusion), channel_id=1, source_target_pairs={{0,3},{1,4},{2,5},{3,6},{4,7},{5,8},{6,9},{7,10},{8,11},{9,12},{10... | collective-permute-start | bytes 884744
  362.0 42.1 %collective-permute-start.4 = (bf16[24,6144]{1,0:T(8,128)(2,1)S(1)}, bf16[24,6144]{1,0:T(8,128)(2,1)}, u32[]{:S(2)}, u32[]{:S(2)}) collective-permute-start(bf16[24,6144]{1,0:T(8,128)(2,1)S(1)} %fusion), channel_id=1, source_target_pairs={{0,4},{1,5},{2,6},{3,7},{4,8},{5,9},{6,10},{7,11},{8,12},{9,13},{1... | collective-permute-start | bytes 884744
  375.7 14.2 %copy-start.4 = (bf16[18,6144]{1,0:T(8,128)(2,1)}, bf16[18,6144]{1,0:T(8,128)(2,1)S(1)}, u32[]{:S(2)}) copy-start(bf16[18,6144]{1,0:T(8,128)(2,1)S(1)} %collective-permute-done.8) | copy-start | bytes 663556
  375.7 34.8 %collective-permute-start.5 = (bf16[24,6144]{1,0:T(8,128)(2,1)S(1)}, bf16[24,6144]{1,0:T(8,128)(2,1)}, u32[]{:S(2)}, u32[]{:S(2)}) collective-permute-start(bf16[24,6144]{1,0:T(8,128)(2,1)S(1)} %fusion), channel_id=1, source_target_pairs={{0,5},{1,6},{2,7},{3,8},{4,9},{5,10},{6,11},{7,12},{8,13},{9,14},{... | collective-permute-start | bytes 884744
  379.9 2.0 copy-start.2
  379.9 36.9 %collective-permute-start.6 = (bf16[24,6144]{1,0:T(8,128)(2,1)S(1)}, bf16[24,6144]{1,0:T(8,128)(2,1)}, u32[]{:S(2)}, u32[]{:S(2)}) collective-permute-start(bf16[24,6144]{1,0:T(8,128)(2,1)S(1)} %fusion), channel_id=1, source_target_pairs={{0,6},{1,7},{2,8},{3,9},{4,10},{5,11},{6,12},{7,13},{8,14},{9,15},... | collective-permute-start | bytes 884744
  381.8 8.1 %copy-start.3 = (bf16[24,6144]{1,0:T(8,128)(2,1)}, bf16[24,6144]{1,0:T(8,128)(2,1)S(1)}, u32[]{:S(2)}) copy-start(bf16[24,6144]{1,0:T(8,128)(2,1)S(1)} %collective-permute-done.2) | copy-start | bytes 884740
  381.8 41.2 %collective-permute-start.7 = (bf16[24,6144]{1,0:T(8,128)(2,1)S(1)}, bf16[24,6144]{1,0:T(8,128)(2,1)}, u32[]{:S(2)}, u32[]{:S(2)}) collective-permute-start(bf16[24,6144]{1,0:T(8,128)(2,1)S(1)} %fusion), channel_id=1, source_target_pairs={{0,7},{1,8},{2,9},{3,10},{4,11},{5,12},{6,13},{7,14},{8,15},{9,16}... | collective-permute-start | bytes 884744
  459.1 24.0 %collective-permute-start = (bf16[64,6144]{1,0:T(8,128)(2,1)S(1)}, bf16[64,6144]{1,0:T(8,128)(2,1)S(1)}, u32[]{:S(2)}, u32[]{:S(2)}) collective-permute-start(bf16[64,6144]{1,0:T(8,128)(2,1)S(1)} %fusion.2), channel_id=1, source_target_pairs={{0,32},{32,64},{64,96},{96,128},{128,160},{160,192},{192,224},{224... | collective-permute-start | bytes 2359304 | tf_op jit(solution)/shard_map/ppermute | solution.py:19
